TPU v7x, 512 devices: a whole 4x4x16 slice. The times are simulated.
512 devices in a mesh: dp: 8 (over x, y_lo), tm: 64 (over z, y_hi, core).
Axes of the slice: x: 4, y: 4 (y_hi: 2, y_lo: 2; y = y_hi * 2 + y_lo), z: 16, core: 2. Of those that a mesh axis runs over, the one named last changes fastest.
Arguments:
- features: bfloat16 [8, 8192, 1536], P('dp', 'tm'), may hold values from -8 to 8
- start_noise: bfloat16 [8, 8192, 1536], P('dp', 'tm'), may hold values from -1 to 1
- cotangent: bfloat16 [8, 8192, 1536], P('dp', 'tm'), may hold values from -0.0234375 to 0.0234375
- in_weight: bfloat16 [3072, 1536], P('tm'), may hold values from -0.15625 to 0.15625
- kernel: float32 [31, 1536], replicated, may hold values from -1 to 1
- bn_gain: float32 [1536], replicated, may hold values from 0.25 to 1.75
- bn_shift: float32 [1536], replicated, may hold values from -1 to 1
- ends: int32 [8], replicated, may hold values from 4096 to 8192
Outputs:
- perturbation: float32 [8, 8192, 1536], P('dp', 'tm')
- grad_kernel: float32 [31, 1536], P(None, 'tm')
- grad_norm: float32 [2, 1536], P(None, 'tm')
Inputs may be any that keep to these rules, and one draw needn't show every extreme that they name: `ends`: frames at or after an utterance's end are padding.
All inputs are finite; a program needn't handle non-finite values.
Results may differ from a plain program's by a relative error of at most 0.0059.
Values may be sent and summed in bfloat16 or wider, within the bound.
A program may use at most 128 MiB of HBM per device.

v0:
```python
import jax
import jax.numpy as jnp
from jax import lax
from jax.sharding import PartitionSpec as P

ASCENT = 2
noise_scale = 0.5
ascent_rate = 0.5
layer_epsilon = 1e-05
batch_epsilon = 1e-05
ascent_epsilon = 1e-06


def normalize(summed):
    centre = summed - jnp.mean(summed, axis=-1, keepdims=True)
    inverse = lax.rsqrt(jnp.mean(centre * centre, axis=-1, keepdims=True) + layer_epsilon)
    return (centre * inverse, inverse)


def lane_conv_forward(padded, kernel, out_length):
    result = jnp.zeros((padded.shape[0], out_length), jnp.float32)
    for offset in range(kernel.shape[0]):
        result = result + kernel[offset][:, None] * padded[:, offset : offset + out_length].astype(
            jnp.float32
        )
    return result


def lane_conv_input_grad(padded, kernel, out_length):
    tap_span = kernel.shape[0] - 1
    result = jnp.zeros((padded.shape[0], out_length), jnp.float32)
    for offset in range(kernel.shape[0]):
        start_col = tap_span - offset
        result = result + kernel[offset][:, None] * padded[
            :, start_col : start_col + out_length
        ].astype(jnp.float32)
    return result


def lane_kernel_grad(grad_bf, padded, out_length):
    grad_float = grad_bf.astype(jnp.float32)
    rows_list = []
    for offset in range(padded.shape[1] - out_length + 1):
        rows_list.append(
            jnp.sum(
                grad_float * padded[:, offset : offset + out_length].astype(jnp.float32), axis=1
            )
        )
    return jnp.stack(rows_list)


def reduce_kernel(partial_grad):
    return lax.psum(partial_grad, "dp")


def on_device(features, start_noise, cotangent, in_weight, kernel, bn_gain, bn_shift, ends):
    frame_rows = features.shape[1]
    model_width = features.shape[2]
    tap_count = kernel.shape[0]
    half_span = (tap_count - 1) // 2
    shard_count = lax.axis_size("tm")
    shard_index = lax.axis_index("tm")
    group_index = lax.axis_index("dp")
    slice_width = model_width // shard_count
    all_frames = frame_rows * shard_count
    utter_end = lax.dynamic_index_in_dim(ends, group_index, 0, keepdims=False)
    live_count = jnp.sum(ends).astype(jnp.float32)
    utter_length = utter_end.astype(jnp.float32)
    frame_ids = shard_index * frame_rows + jnp.arange(frame_rows, dtype=jnp.int32)
    live_frames = (frame_ids < utter_end).astype(jnp.float32)
    live_whole = (jnp.arange(all_frames, dtype=jnp.int32) < utter_end).astype(jnp.float32)
    channel_start = shard_index * slice_width
    kernel_slice = lax.dynamic_slice_in_dim(kernel, channel_start, slice_width, 1)
    gain_slice = lax.dynamic_slice_in_dim(bn_gain, channel_start, slice_width, 0)
    shift_slice = lax.dynamic_slice_in_dim(bn_shift, channel_start, slice_width, 0)
    weight_full = lax.all_gather(in_weight, "tm", axis=0, tiled=True)
    inputs = features[0].astype(jnp.float32)
    perturbation = noise_scale * start_noise[0].astype(jnp.float32) * live_frames[:, None]
    cot_channels = lax.all_to_all(
        jnp.transpose(cotangent[0])[None], "tm", split_axis=1, concat_axis=2, tiled=True
    )[0]
    upstream = live_whole[None, :] * cot_channels.astype(jnp.float32) / ASCENT
    kernel_total = jnp.zeros((tap_count, slice_width), jnp.float32)
    norm_total = jnp.zeros((2, slice_width), jnp.float32)
    for ascent_step in range(ASCENT):
        summed = inputs + perturbation
        normed, inverse = normalize(summed)
        hidden = lax.dot_general(
            normed.astype(jnp.bfloat16),
            weight_full,
            (((1,), (1,)), ((), ())),
            preferred_element_type=jnp.float32,
        )
        value_half = hidden[:, :model_width]
        gate_half = jax.nn.sigmoid(hidden[:, model_width:])
        glu = (value_half * gate_half * live_frames[:, None]).astype(jnp.bfloat16)
        glu_local = lax.all_to_all(
            jnp.transpose(glu)[None], "tm", split_axis=1, concat_axis=2, tiled=True
        )[0]
        padded = jnp.pad(glu_local, ((0, 0), (half_span, half_span)))
        conv_out = lane_conv_forward(padded, kernel_slice, all_frames)
        live_mask = live_whole[None, :]
        batch_mean = lax.psum(jnp.sum(live_mask * conv_out, axis=1), "dp") / live_count
        centred = conv_out - batch_mean[:, None]
        variance = lax.psum(jnp.sum(live_mask * centred * centred, axis=1), "dp") / live_count
        inv_std = lax.rsqrt(variance + batch_epsilon)[:, None]
        gain_now, shift_now = (gain_slice[:, None], shift_slice[:, None])
        scaled = centred * inv_std
        pre_act = gain_now * scaled + shift_now
        pre_sigmoid = jax.nn.sigmoid(pre_act)
        grad_pre = upstream * pre_sigmoid * (1.0 + pre_act * (1.0 - pre_sigmoid))
        shift_sum, gain_sum = lax.psum(
            (jnp.sum(grad_pre, axis=1), jnp.sum(grad_pre * scaled, axis=1)), "dp"
        )
        norm_total = norm_total + jnp.stack([gain_sum, shift_sum])
        grad_conv = (
            live_mask
            * inv_std
            * gain_now
            * (grad_pre - (shift_sum[:, None] + scaled * gain_sum[:, None]) / live_count)
        ).astype(jnp.bfloat16)
        kernel_part = lane_kernel_grad(grad_conv, padded, all_frames)
        kernel_total = kernel_total + reduce_kernel(kernel_part)
        if ascent_step + 1 < ASCENT:
            grad_pad = jnp.pad(grad_conv, ((0, 0), (half_span, half_span)))
            grad_local = (
                lane_conv_input_grad(grad_pad, kernel_slice, all_frames) * live_mask
            ).astype(jnp.bfloat16)
            grad_glu = jnp.transpose(
                lax.all_to_all(grad_local[None], "tm", split_axis=2, concat_axis=1, tiled=True)[0]
            )
            grad_float = grad_glu.astype(jnp.float32)
            grad_hidden = jnp.concatenate(
                [grad_float * gate_half, grad_float * value_half * gate_half * (1.0 - gate_half)],
                axis=1,
            ).astype(jnp.bfloat16)
            grad_normed = jnp.dot(grad_hidden, weight_full, preferred_element_type=jnp.float32)
            grad_sum = inverse * (
                grad_normed
                - jnp.mean(grad_normed, axis=-1, keepdims=True)
                - normed * jnp.mean(grad_normed * normed, axis=-1, keepdims=True)
            )
            direction = live_frames[:, None] * grad_sum
            square_total = lax.psum(jnp.sum(direction * direction), "tm")
            perturbation = perturbation + direction * (
                ascent_rate
                * jnp.sqrt(utter_length * model_width)
                / (jnp.sqrt(square_total) + ascent_epsilon)
            )
    return (perturbation[None], kernel_total, norm_total)


def solution(mesh):
    return jax.shard_map(
        on_device,
        mesh=mesh,
        in_specs=(
            P("dp", "tm", None),
            P("dp", "tm", None),
            P("dp", "tm", None),
            P("tm", None),
            P(),
            P(),
            P(),
            P(),
        ),
        out_specs=(P("dp", "tm", None), P(None, "tm"), P(None, "tm")),
        check_vma=False,
    )
```

profile of v0, /device:TPU:16, one launch (start us, length us, event | category | flops | bytes accessed | tf_op | source)
XLA Modules:
  0.0 742.7 jit_solution(14522599243444606599)
XLA Ops:
  15.8 8.8 %reduce.1 = bf16[1536,128]{1,0:T(8,128)(2,1)S(1)} reduce(bf16[1536,1,128]{2,1,0:T(2,128)(2,1)S(1)} %bitcast.268, bf16[]{:T(256)} %broadcast.129), dimensions={1}, to_apply=%bitcast.247.reduce_sub_computation | reduce | bytes 786434
  25.5 18.9 %all-to-all-start.1 = ((bf16[64,2,1536]{2,1,0:T(2,128)(2,1)}), bf16[64,2,1536]{2,1,0:T(2,128)(2,1)S(1)}, u32[]{:S(2)}, u32[]{:S(2)}) async-start(bf16[64,2,1536]{2,1,0:T(2,128)(2,1)} %reshape.112), calls=%async_computation.1 | async-start | bytes 786432 | tf_op jit(solution)/shard_map/all_to_all | solution.py:79
  47.0 140.4 %all-gather.2.cloned.1.call-done = bf16[3072,1536]{1,0:T(8,128)(2,1)} async-done(((bf16[48,1536]{1,0:T(8,128)(2,1)}), bf16[3072,1536]{1,0:T(8,128)(2,1)}) %all-gather.2.cloned.1.call-update) | async-done | bytes 9437200 | tf_op jit(solution)/shard_map/all_gather | solution.py:76
  187.4 6.9 fusion.162
  197.5 9.5 %reduce = bf16[1536,128]{1,0:T(8,128)(2,1)} reduce(bf16[1536,1,128]{2,1,0:T(2,128)(2,1)S(1)} %bitcast.270, bf16[]{:T(256)} %broadcast.129), dimensions={1}, to_apply=%bitcast.227.reduce_sub_computation | reduce | bytes 786434
  208.8 11.1 %all-to-all-start = ((bf16[64,2,1536]{2,1,0:T(2,128)(2,1)}), bf16[64,2,1536]{2,1,0:T(2,128)(2,1)}, u32[]{:S(2)}, u32[]{:S(2)}) async-start(bf16[64,2,1536]{2,1,0:T(2,128)(2,1)} %reshape.114), calls=%async_computation | async-start | bytes 786432 | tf_op jit(solution)/shard_map/all_to_all | solution.py:97
  230.5 17.4 %all-to-all-done = bf16[64,2,1536]{2,1,0:T(2,128)(2,1)} async-done(((bf16[64,2,1536]{2,1,0:T(2,128)(2,1)}), bf16[64,2,1536]{2,1,0:T(2,128)(2,1)}, u32[]{:S(2)}, u32[]{:S(2)}) %all-to-all-start) | async-done | bytes 393248 | tf_op jit(solution)/shard_map/all_to_all | solution.py:97
  257.5 20.7 %psum.77 = f32[24]{0:T(128)} all-reduce(f32[24]{0:T(128)} %get-tuple-element.100), channel_id=1, replica_groups=mesh['dp'=8,'tm'=64] {'dp'}, use_global_device_ids=true, to_apply=%region_3.4 | all-reduce | flops 24 | bytes 192 | tf_op jit(solution)/shard_map/psum | solution.py:103
  281.0 16.6 %psum.78 = f32[24]{0:T(128)} all-reduce(f32[24]{0:T(128)} %fusion.60), channel_id=1, replica_groups=mesh['dp'=8,'tm'=64] {'dp'}, use_global_device_ids=true, to_apply=%region_6.7 | all-reduce | flops 24 | bytes 192 | tf_op jit(solution)/shard_map/psum | solution.py:105
  302.2 18.9 %all-reduce.4 = (f32[24]{0:T(128)}, f32[24]{0:T(128)}) all-reduce(f32[24]{0:T(128)} %get-tuple-element.83, f32[24]{0:T(128)} %get-tuple-element.82), channel_id=1, replica_groups=mesh['dp'=8,'tm'=64] {'dp'}, use_global_device_ids=true, to_apply=%region_10.11 | all-reduce | flops 48 | bytes 384 | tf_op jit(solution)/shard_map/psum | solution.py:112
  330.4 6.7 copy.52
  337.1 46.5 %reduce.2 = bf16[8192,24]{1,0:T(8,128)(2,1)} reduce(bf16[8192,1,24]{2,1,0:T(2,128)(2,1)} %bitcast.248, bf16[]{:T(256)} %broadcast.129), dimensions={1}, to_apply=%bitcast.229.reduce_sub_computation | reduce | bytes 786434
  395.2 27.1 %all-to-all-done.2 = bf16[64,2,1536]{2,1,0:T(2,128)(2,1)S(1)} async-done(((bf16[64,2,1536]{2,1,0:T(2,128)(2,1)}), bf16[64,2,1536]{2,1,0:T(2,128)(2,1)S(1)}, u32[]{:S(2)}, u32[]{:S(2)}) %all-to-all-start.2) | async-done | bytes 393248 | tf_op jit(solution)/shard_map/all_to_all | solution.py:130
  422.3 8.9 %reshape.117 = bf16[8192,1,24]{2,1,0:T(2,128)(2,1)} reshape(bf16[64,2,1536]{2,1,0:T(2,128)(2,1)S(1)} %all-to-all-done.2) | data formatting | bytes 786432
  431.2 8.0 %copy.53 = bf16[1,24,8192]{2,1,0:T(8,128)(2,1)S(1)} copy(bf16[1,24,8192]{1,0,2:T(2,128)(2,1)} %bitcast.249) | data formatting | bytes 786432 | tf_op jit(solution)/shard_map/all_to_all | solution.py:130
  449.0 125.4 %psum.81 = f32[]{:T(128)} all-reduce(f32[]{:T(128)} %get-tuple-element.97), channel_id=1, replica_groups=mesh['dp'=8,'tm'=64] {'tm'}, use_global_device_ids=true, to_apply=%region_14.15 | all-reduce | flops 1 | bytes 8 | tf_op jit(solution)/shard_map/psum | solution.py:144
  576.5 6.8 fusion.165
  584.2 8.8 %reduce.3 = bf16[1536,128]{1,0:T(8,128)(2,1)S(1)} reduce(bf16[1536,1,128]{2,1,0:T(2,128)(2,1)S(1)} %bitcast.269, bf16[]{:T(256)} %broadcast.129), dimensions={1}, to_apply=%bitcast.231.reduce_sub_computation | reduce | bytes 786434
  593.8 11.3 %all-to-all-start.3 = ((bf16[64,2,1536]{2,1,0:T(2,128)(2,1)}), bf16[64,2,1536]{2,1,0:T(2,128)(2,1)S(1)}, u32[]{:S(2)}, u32[]{:S(2)}) async-start(bf16[64,2,1536]{2,1,0:T(2,128)(2,1)} %reshape.118), calls=%async_computation.3 | async-start | bytes 786432 | tf_op jit(solution)/shard_map/all_to_all | solution.py:97
  609.0 24.0 %all-to-all-done.3 = bf16[64,2,1536]{2,1,0:T(2,128)(2,1)S(1)} async-done(((bf16[64,2,1536]{2,1,0:T(2,128)(2,1)}), bf16[64,2,1536]{2,1,0:T(2,128)(2,1)S(1)}, u32[]{:S(2)}, u32[]{:S(2)}) %all-to-all-start.3) | async-done | bytes 393248 | tf_op jit(solution)/shard_map/all_to_all | solution.py:97
  639.8 16.1 %psum.83 = f32[24]{0:T(128)S(1)} all-reduce(f32[24]{0:T(128)} %get-tuple-element.92), channel_id=1, replica_groups=mesh['dp'=8,'tm'=64] {'dp'}, use_global_device_ids=true, to_apply=%region_50.51 | all-reduce | flops 24 | bytes 192 | tf_op jit(solution)/shard_map/psum | solution.py:103
  656.9 18.0 %psum.84 = f32[24]{0:T(128)S(1)} all-reduce(f32[24]{0:T(128)S(1)} %fusion.61), channel_id=1, replica_groups=mesh['dp'=8,'tm'=64] {'dp'}, use_global_device_ids=true, to_apply=%region_52.53 | all-reduce | flops 24 | bytes 192 | tf_op jit(solution)/shard_map/psum | solution.py:105
  678.1 16.3 %all-reduce.3 = (f32[24]{0:T(128)S(1)}, f32[24]{0:T(128)S(1)}) all-reduce(f32[24]{0:T(128)} %get-tuple-element.49, f32[24]{0:T(128)} %get-tuple-element.48), channel_id=1, replica_groups=mesh['dp'=8,'tm'=64] {'dp'}, use_global_device_ids=true, to_apply=%region_56.57 | all-reduce | flops 48 | bytes 384 | tf_op jit(solution)/shard_map/psum | solution.py:112
  701.9 32.5 %psum.88 = f32[31,24]{1,0:T(8,128)S(1)} all-reduce(f32[31,24]{1,0:T(8,128)S(1)} %add.520), channel_id=1, replica_groups=mesh['dp'=8,'tm'=64] {'dp'}, use_global_device_ids=true, to_apply=%region_46.47 | all-reduce | flops 744 | bytes 5952 | tf_op jit(solution)/shard_map/psum | solution.py:53
  (170 shorter events, 99.9 us)
Async XLA Ops:
  7.2 37.2 %copy-start.46 = (s32[8]{0:T(128)S(1)}, s32[8]{0:T(128)}, u32[]{:S(2)}) copy-start(s32[8]{0:T(128)} %param.15) | copy-start | bytes 100
  7.2 38.5 %copy-start.1 = (bf16[1,128,1536]{2,1,0:T(8,128)(2,1)S(1)}, bf16[1,128,1536]{2,1,0:T(8,128)(2,1)}, u32[]{:S(2)}) copy-start(bf16[1,128,1536]{2,1,0:T(8,128)(2,1)} %param.8) | copy-start | bytes 1179652
  7.2 38.5 %copy-start = (bf16[1,128,1536]{2,1,0:T(8,128)(2,1)S(1)}, bf16[1,128,1536]{2,1,0:T(8,128)(2,1)}, u32[]{:S(2)}) copy-start(bf16[1,128,1536]{2,1,0:T(8,128)(2,1)} %param.9) | copy-start | bytes 1179652
  7.2 180.2 %all-gather.2.cloned.1.call-start = ((), (), s32[]{:S(2)}) async-start(), calls=%async_computation.4 | async-start | bytes 9584640 | tf_op jit(solution)/shard_map/all_gather | solution.py:76
  25.5 183.3 %all-to-all-start.1 = ((bf16[64,2,1536]{2,1,0:T(2,128)(2,1)}), bf16[64,2,1536]{2,1,0:T(2,128)(2,1)S(1)}, u32[]{:S(2)}, u32[]{:S(2)}) async-start(bf16[64,2,1536]{2,1,0:T(2,128)(2,1)} %reshape.112), calls=%async_computation.1 | async-start | bytes 786432 | tf_op jit(solution)/shard_map/all_to_all | solution.py:79
  46.0 148.3 %copy-start.11 = (f32[128]{0:T(128)}, f32[128]{0:T(128)S(1)}, u32[]{:S(2)}) copy-start(f32[128]{0:T(128)S(1)} %broadcast_multiply_fusion.3) | copy-start | bytes 1540
  46.6 147.7 %copy-start.8 = (f32[128]{0:T(128)}, f32[128]{0:T(128)S(1)}, u32[]{:S(2)}) copy-start(f32[128]{0:T(128)S(1)} %compare_convert_fusion) | copy-start | bytes 1540
  47.0 147.3 %copy-start.40 = (f32[128]{0:T(128)}, f32[128]{0:T(128)S(1)}, u32[]{:S(2)}) copy-start(f32[128]{0:T(128)S(1)} %add_rsqrt_fusion.3) | copy-start | bytes 1540
  208.8 39.0 %all-to-all-start = ((bf16[64,2,1536]{2,1,0:T(2,128)(2,1)}), bf16[64,2,1536]{2,1,0:T(2,128)(2,1)}, u32[]{:S(2)}, u32[]{:S(2)}) async-start(bf16[64,2,1536]{2,1,0:T(2,128)(2,1)} %reshape.114), calls=%async_computation | async-start | bytes 786432 | tf_op jit(solution)/shard_map/all_to_all | solution.py:97
  388.5 33.8 %all-to-all-start.2 = ((bf16[64,2,1536]{2,1,0:T(2,128)(2,1)}), bf16[64,2,1536]{2,1,0:T(2,128)(2,1)S(1)}, u32[]{:S(2)}, u32[]{:S(2)}) async-start(bf16[64,2,1536]{2,1,0:T(2,128)(2,1)} %reshape.116), calls=%async_computation.2 | async-start | bytes 786432 | tf_op jit(solution)/shard_map/all_to_all | solution.py:130
  584.2 49.6 %copy-start.7 = (f32[24]{0:T(128)S(1)}, f32[24]{0:T(128)}, u32[]{:S(2)}) copy-start(f32[24]{0:T(128)} %get-tuple-element.108) | copy-start | bytes 292
  593.8 81.0 %copy-start.4 = (f32[1,24,64,128]{3,2,1,0:T(8,128)S(1)}, f32[1,24,64,128]{3,2,1,0:T(8,128)}, u32[]{:S(2)}) copy-start(f32[1,24,64,128]{3,2,1,0:T(8,128)} %copy.51) | copy-start | bytes 2359300
  593.8 39.2 %all-to-all-start.3 = ((bf16[64,2,1536]{2,1,0:T(2,128)(2,1)}), bf16[64,2,1536]{2,1,0:T(2,128)(2,1)S(1)}, u32[]{:S(2)}, u32[]{:S(2)}) async-start(bf16[64,2,1536]{2,1,0:T(2,128)(2,1)} %reshape.118), calls=%async_computation.3 | async-start | bytes 786432 | tf_op jit(solution)/shard_map/all_to_all | solution.py:97
  633.7 66.2 %copy-start.6 = (bf16[1,24,64,128]{3,2,1,0:T(8,128)(2,1)S(1)}, bf16[1,24,64,128]{3,2,1,0:T(8,128)(2,1)}, u32[]{:S(2)}) copy-start(bf16[1,24,64,128]{3,2,1,0:T(8,128)(2,1)} %copy-done.5) | copy-start | bytes 1179652
  674.9 26.6 %copy-start.13 = (f32[24]{0:T(128)S(1)}, f32[24]{0:T(128)}, u32[]{:S(2)}) copy-start(f32[24]{0:T(128)} %get-tuple-element.50) | copy-start | bytes 292
  674.9 26.6 %copy-start.14 = (f32[24]{0:T(128)S(1)}, f32[24]{0:T(128)}, u32[]{:S(2)}) copy-start(f32[24]{0:T(128)} %get-tuple-element.51) | copy-start | bytes 292
  674.9 26.6 %copy-start.15 = (f32[24]{0:T(128)S(1)}, f32[24]{0:T(128)}, u32[]{:S(2)}) copy-start(f32[24]{0:T(128)} %get-tuple-element.52) | copy-start | bytes 292
  677.9 23.7 %copy-start.19 = (f32[24]{0:T(128)S(1)}, f32[24]{0:T(128)}, u32[]{:S(2)}) copy-start(f32[24]{0:T(128)} %get-tuple-element.56) | copy-start | bytes 292
  677.9 23.7 %copy-start.20 = (f32[24]{0:T(128)S(1)}, f32[24]{0:T(128)}, u32[]{:S(2)}) copy-start(f32[24]{0:T(128)} %get-tuple-element.57) | copy-start | bytes 292
  677.9 23.7 %copy-start.21 = (f32[24]{0:T(128)S(1)}, f32[24]{0:T(128)}, u32[]{:S(2)}) copy-start(f32[24]{0:T(128)} %get-tuple-element.58) | copy-start | bytes 292
  677.9 23.7 %copy-start.22 = (f32[24]{0:T(128)S(1)}, f32[24]{0:T(128)}, u32[]{:S(2)}) copy-start(f32[24]{0:T(128)} %get-tuple-element.59) | copy-start | bytes 292
  677.9 23.7 %copy-start.23 = (f32[24]{0:T(128)S(1)}, f32[24]{0:T(128)}, u32[]{:S(2)}) copy-start(f32[24]{0:T(128)} %get-tuple-element.60) | copy-start | bytes 292
  678.1 56.9 %copy-start.44 = (f32[24]{0:T(128)S(1)}, f32[24]{0:T(128)}, u32[]{:S(2)}) copy-start(f32[24]{0:T(128)} %get-tuple-element.88) | copy-start | bytes 292
  678.1 56.9 %copy-start.45 = (f32[24]{0:T(128)S(1)}, f32[24]{0:T(128)}, u32[]{:S(2)}) copy-start(f32[24]{0:T(128)} %get-tuple-element.89) | copy-start | bytes 292
  (28 other events, 493.6 us)
Sparse Core Ops, SparseCore 0:
  11.3 176.0 all-gather.1
where the time goes:
time: 750 us; the launch traced here: 743 us
  blocking collectives  264 us (35%)
  waiting for transfers between devices  210 us (28%)
  other arithmetic  125 us (17%)
  local copies, waits for them, and re-layouts  60.1 us (8%)
  starting transfers between devices  47.4 us (6%)
  matrix products  19 us (3%)
  between operations  17.2 us (2%)
    all_gather x1, waiting for transfers between devices, on_device(): weight_full = lax.all_gather(in_weight, 'tm', axis=0, tiled=True)  140 us
    psum x1, blocking collectives, on_device(): square_total = lax.psum(jnp.sum(direction * direction), 'tm')  125 us
    unnamed x5, other arithmetic  73.6 us
    all_to_all x2, waiting for transfers between devices, on_device(): lax.all_to_all(jnp.transpose(glu)[None], 'tm', split_axis=1, concat_axis=...  41.4 us
    psum x2, blocking collectives, on_device(): lax.psum(jnp.sum(live_mask * conv_out, axis=1), 'dp') / live_count  36.8 us
    psum x2, blocking collectives, on_device(): lax.psum((jnp.sum(grad_pre, axis=1), jnp.sum(grad_pre * scaled, axis=1)),...  35.2 us
    psum x2, blocking collectives, on_device(): lax.psum(jnp.sum(live_mask * centred * centred, axis=1), 'dp') / live_count  34.5 us
    psum x1, blocking collectives, reduce_kernel(): return lax.psum(partial_grad, 'dp')  32.5 us
  transfers between devices with their start and end apart: 5, of which 4 were waited for; matrix products, arithmetic and copies ran while one was open for 7% of the time, Pallas kernels for 0%

commit v1 on v0

--- a/solution.py
+++ b/solution.py
@@ -2,6 +2,7 @@
 import jax.numpy as jnp
 from jax import lax
 from jax.sharding import PartitionSpec as P
+from jax.lax import all_to_all, axis_size
 
 ASCENT = 2
 noise_scale = 0.5
@@ -9,6 +10,11 @@
 layer_epsilon = 1e-05
 batch_epsilon = 1e-05
 ascent_epsilon = 1e-06
+
+
+def review_links_over_axis(xin):
+    y_new = jnp.stack([xin for _ in range(axis_size("tm"))], axis=0)
+    return jnp.concatenate(all_to_all(y_new, "tm", 0, 0), axis=0)
 
 
 def normalize(summed):
@@ -73,7 +79,7 @@
     kernel_slice = lax.dynamic_slice_in_dim(kernel, channel_start, slice_width, 1)
     gain_slice = lax.dynamic_slice_in_dim(bn_gain, channel_start, slice_width, 0)
     shift_slice = lax.dynamic_slice_in_dim(bn_shift, channel_start, slice_width, 0)
-    weight_full = lax.all_gather(in_weight, "tm", axis=0, tiled=True)
+    weight_full = review_links_over_axis(in_weight)
     inputs = features[0].astype(jnp.float32)
     perturbation = noise_scale * start_noise[0].astype(jnp.float32) * live_frames[:, None]
     cot_channels = lax.all_to_all(

time: 750 us -> 1010 us (1.35)
  waiting for transfers between devices: 210 us -> 471 us
  between operations: 17.2 us -> 3.85 us
    all_to_all x0 -> x1, waiting for transfers between devices: none -> 397 us  [review_links_over_axis(): return jnp.concatenate(all_to_all(y_new, 'tm', 0, 0), axis=0)]
    all_gather x1 -> x0, waiting for transfers between devices: 140 us -> none  [on_device(): weight_full = lax.all_gather(in_weight, 'tm', axis=0, tiled=True)]
    all_to_all x0 -> x1, starting transfers between devices: none -> 18.9 us  [review_links_over_axis(): return jnp.concatenate(all_to_all(y_new, 'tm', 0, 0), axis=0)]
    all_to_all x1, starting transfers between devices: 18.9 us -> 5.65 us  [on_device(): lax.all_to_all(jnp.transpose(cotangent[0])[None], 'tm', split_axis=1, con...]
    unnamed x110 -> x112, local copies, waits for them, and re-layouts: 26.4 us -> 25.5 us
  transfers between devices with their start and end apart: 5 -> 5, of which waited for: 4 -> 5; matrix products, arithmetic and copies ran while one was open for 7% -> 5% of each run, Pallas kernels for 0% -> 0%
where the time goes in v1:
time: 1010 us; the launch traced here: 999 us
  waiting for transfers between devices  471 us (47%)
  blocking collectives  264 us (26%)
  other arithmetic  125 us (12%)
  local copies, waits for them, and re-layouts  64.5 us (6%)
  starting transfers between devices  51.8 us (5%)
  matrix products  19 us (2%)
    all_to_all x1, waiting for transfers between devices, review_links_over_axis(): return jnp.concatenate(all_to_all(y_new, 'tm', 0, 0), axis=0)  397 us
    psum x1, blocking collectives, on_device(): square_total = lax.psum(jnp.sum(direction * direction), 'tm')  125 us
    unnamed x5, other arithmetic  73.9 us
    all_to_all x2, waiting for transfers between devices, on_device(): lax.all_to_all(jnp.transpose(glu)[None], 'tm', split_axis=1, concat_axis=...  41.6 us
    psum x2, blocking collectives, on_device(): lax.psum(jnp.sum(live_mask * conv_out, axis=1), 'dp') / live_count  36.1 us
    psum x2, blocking collectives, on_device(): lax.psum((jnp.sum(grad_pre, axis=1), jnp.sum(grad_pre * scaled, axis=1)),...  35.2 us
    psum x2, blocking collectives, on_device(): lax.psum(jnp.sum(live_mask * centred * centred, axis=1), 'dp') / live_count  34.5 us
    psum x1, blocking collectives, reduce_kernel(): return lax.psum(partial_grad, 'dp')  32.5 us
  transfers between devices with their start and end apart: 5, of which 5 were waited for; matrix products, arithmetic and copies ran while one was open for 5% of the time, Pallas kernels for 0%

profile of v1, /device:TPU:16, one launch (start us, length us, event | category | flops | bytes accessed | tf_op | source)
XLA Modules:
  0.0 999.5 jit_solution(7381033206506379327)
XLA Ops:
  6.3 18.9 %all-to-all-start = ((bf16[64,48,1536]{2,1,0:T(8,128)(2,1)}), bf16[64,48,1536]{2,1,0:T(8,128)(2,1)}, u32[]{:S(2)}, u32[]{:S(2)}) async-start(bf16[64,48,1536]{2,1,0:T(8,128)(2,1)} %stack.277), calls=%async_computation | async-start | bytes 18874368 | tf_op jit(solution)/shard_map/all_to_all | solution.py:17
  32.2 8.8 reduce.1
  43.5 397.3 %all-to-all-done = bf16[64,48,1536]{2,1,0:T(8,128)(2,1)} async-done(((bf16[64,48,1536]{2,1,0:T(8,128)(2,1)}), bf16[64,48,1536]{2,1,0:T(8,128)(2,1)}, u32[]{:S(2)}, u32[]{:S(2)}) %all-to-all-start) | async-done | bytes 9437216 | tf_op jit(solution)/shard_map/all_to_all | solution.py:17
  447.5 6.9 fusion.171
  457.6 9.6 reduce
  474.3 10.0 all-to-all-start.1
  494.5 17.6 %all-to-all-done.1 = bf16[64,2,1536]{2,1,0:T(2,128)(2,1)} async-done(((bf16[64,2,1536]{2,1,0:T(2,128)(2,1)}), bf16[64,2,1536]{2,1,0:T(2,128)(2,1)}, u32[]{:S(2)}, u32[]{:S(2)}) %all-to-all-start.1) | async-done | bytes 393248 | tf_op jit(solution)/shard_map/all_to_all | solution.py:103
  521.8 20.0 %psum.77 = f32[24]{0:T(128)} all-reduce(f32[24]{0:T(128)} %get-tuple-element.100), channel_id=1, replica_groups=mesh['dp'=8,'tm'=64] {'dp'}, use_global_device_ids=true, to_apply=%region_3.4 | all-reduce | flops 24 | bytes 192 | tf_op jit(solution)/shard_map/psum | solution.py:109
  544.6 16.6 %psum.78 = f32[24]{0:T(128)} all-reduce(f32[24]{0:T(128)} %fusion.67), channel_id=1, replica_groups=mesh['dp'=8,'tm'=64] {'dp'}, use_global_device_ids=true, to_apply=%region_6.7 | all-reduce | flops 24 | bytes 192 | tf_op jit(solution)/shard_map/psum | solution.py:111
  565.8 18.9 %all-reduce.4 = (f32[24]{0:T(128)}, f32[24]{0:T(128)}) all-reduce(f32[24]{0:T(128)} %get-tuple-element.83, f32[24]{0:T(128)} %get-tuple-element.82), channel_id=1, replica_groups=mesh['dp'=8,'tm'=64] {'dp'}, use_global_device_ids=true, to_apply=%region_10.11 | all-reduce | flops 48 | bytes 384 | tf_op jit(solution)/shard_map/psum | solution.py:118
  594.0 6.7 copy.52
  600.7 46.6 %reduce.2 = bf16[8192,24]{1,0:T(8,128)(2,1)} reduce(bf16[8192,1,24]{2,1,0:T(2,128)(2,1)} %bitcast.267, bf16[]{:T(256)} %broadcast.140), dimensions={1}, to_apply=%bitcast.248.reduce_sub_computation | reduce | bytes 786434
  658.7 27.1 %all-to-all-done.3 = bf16[64,2,1536]{2,1,0:T(2,128)(2,1)S(1)} async-done(((bf16[64,2,1536]{2,1,0:T(2,128)(2,1)}), bf16[64,2,1536]{2,1,0:T(2,128)(2,1)S(1)}, u32[]{:S(2)}, u32[]{:S(2)}) %all-to-all-start.3) | async-done | bytes 393248 | tf_op jit(solution)/shard_map/all_to_all | solution.py:136
  685.9 8.9 reshape.142
  694.8 8.0 copy.53
  712.6 125.4 %psum.81 = f32[]{:T(128)} all-reduce(f32[]{:T(128)} %get-tuple-element.97), channel_id=1, replica_groups=mesh['dp'=8,'tm'=64] {'tm'}, use_global_device_ids=true, to_apply=%region_14.15 | all-reduce | flops 1 | bytes 8 | tf_op jit(solution)/shard_map/psum | solution.py:150
  840.1 6.8 fusion.169
  847.8 8.8 reduce.3
  857.5 11.3 %all-to-all-start.4 = ((bf16[64,2,1536]{2,1,0:T(2,128)(2,1)}), bf16[64,2,1536]{2,1,0:T(2,128)(2,1)S(1)}, u32[]{:S(2)}, u32[]{:S(2)}) async-start(bf16[64,2,1536]{2,1,0:T(2,128)(2,1)} %reshape.143), calls=%async_computation.4 | async-start | bytes 786432 | tf_op jit(solution)/shard_map/all_to_all | solution.py:103
  872.7 24.0 %all-to-all-done.4 = bf16[64,2,1536]{2,1,0:T(2,128)(2,1)S(1)} async-done(((bf16[64,2,1536]{2,1,0:T(2,128)(2,1)}), bf16[64,2,1536]{2,1,0:T(2,128)(2,1)S(1)}, u32[]{:S(2)}, u32[]{:S(2)}) %all-to-all-start.4) | async-done | bytes 393248 | tf_op jit(solution)/shard_map/all_to_all | solution.py:103
  903.4 16.1 %psum.83 = f32[24]{0:T(128)S(1)} all-reduce(f32[24]{0:T(128)} %get-tuple-element.92), channel_id=1, replica_groups=mesh['dp'=8,'tm'=64] {'dp'}, use_global_device_ids=true, to_apply=%region_50.51 | all-reduce | flops 24 | bytes 192 | tf_op jit(solution)/shard_map/psum | solution.py:109
  920.5 18.0 %psum.84 = f32[24]{0:T(128)S(1)} all-reduce(f32[24]{0:T(128)S(1)} %fusion.68), channel_id=1, replica_groups=mesh['dp'=8,'tm'=64] {'dp'}, use_global_device_ids=true, to_apply=%region_52.53 | all-reduce | flops 24 | bytes 192 | tf_op jit(solution)/shard_map/psum | solution.py:111
  941.8 16.3 %all-reduce.3 = (f32[24]{0:T(128)S(1)}, f32[24]{0:T(128)S(1)}) all-reduce(f32[24]{0:T(128)} %get-tuple-element.49, f32[24]{0:T(128)} %get-tuple-element.48), channel_id=1, replica_groups=mesh['dp'=8,'tm'=64] {'dp'}, use_global_device_ids=true, to_apply=%region_56.57 | all-reduce | flops 48 | bytes 384 | tf_op jit(solution)/shard_map/psum | solution.py:118
  965.5 32.5 %psum.88 = f32[31,24]{1,0:T(8,128)S(1)} all-reduce(f32[31,24]{1,0:T(8,128)S(1)} %add.524), channel_id=1, replica_groups=mesh['dp'=8,'tm'=64] {'dp'}, use_global_device_ids=true, to_apply=%region_46.47 | all-reduce | flops 744 | bytes 5952 | tf_op jit(solution)/shard_map/psum | solution.py:59
  (172 shorter events, 114.6 us)
Async XLA Ops:
  6.3 35.6 %copy-start.47 = (s32[8]{0:T(128)S(1)}, s32[8]{0:T(128)}, u32[]{:S(2)}) copy-start(s32[8]{0:T(128)} %param.15) | copy-start | bytes 100
  6.3 434.5 %all-to-all-start = ((bf16[64,48,1536]{2,1,0:T(8,128)(2,1)}), bf16[64,48,1536]{2,1,0:T(8,128)(2,1)}, u32[]{:S(2)}, u32[]{:S(2)}) async-start(bf16[64,48,1536]{2,1,0:T(8,128)(2,1)} %stack.277), calls=%async_computation | async-start | bytes 18874368 | tf_op jit(solution)/shard_map/all_to_all | solution.py:17
  43.5 410.9 %copy-start.12 = (f32[128]{0:T(128)}, f32[128]{0:T(128)S(1)}, u32[]{:S(2)}) copy-start(f32[128]{0:T(128)S(1)} %broadcast_multiply_fusion.3) | copy-start | bytes 1540
  440.8 33.5 %all-to-all-start.2 = ((bf16[64,2,1536]{2,1,0:T(2,128)(2,1)}), bf16[64,2,1536]{2,1,0:T(2,128)(2,1)S(1)}, u32[]{:S(2)}, u32[]{:S(2)}) async-start(bf16[64,2,1536]{2,1,0:T(2,128)(2,1)} %reshape.137), calls=%async_computation.2 | async-start | bytes 786432 | tf_op jit(solution)/shard_map/all_to_all | solution.py:85
  474.3 37.9 %all-to-all-start.1 = ((bf16[64,2,1536]{2,1,0:T(2,128)(2,1)}), bf16[64,2,1536]{2,1,0:T(2,128)(2,1)}, u32[]{:S(2)}, u32[]{:S(2)}) async-start(bf16[64,2,1536]{2,1,0:T(2,128)(2,1)} %reshape.139), calls=%async_computation.1 | async-start | bytes 786432 | tf_op jit(solution)/shard_map/all_to_all | solution.py:103
  652.1 33.8 %all-to-all-start.3 = ((bf16[64,2,1536]{2,1,0:T(2,128)(2,1)}), bf16[64,2,1536]{2,1,0:T(2,128)(2,1)S(1)}, u32[]{:S(2)}, u32[]{:S(2)}) async-start(bf16[64,2,1536]{2,1,0:T(2,128)(2,1)} %reshape.141), calls=%async_computation.3 | async-start | bytes 786432 | tf_op jit(solution)/shard_map/all_to_all | solution.py:136
  847.7 49.6 %copy-start.8 = (f32[24]{0:T(128)S(1)}, f32[24]{0:T(128)}, u32[]{:S(2)}) copy-start(f32[24]{0:T(128)} %get-tuple-element.108) | copy-start | bytes 292
  857.5 81.0 %copy-start.4 = (f32[1,24,64,128]{3,2,1,0:T(8,128)S(1)}, f32[1,24,64,128]{3,2,1,0:T(8,128)}, u32[]{:S(2)}) copy-start(f32[1,24,64,128]{3,2,1,0:T(8,128)} %copy.51) | copy-start | bytes 2359300
  857.5 39.2 %all-to-all-start.4 = ((bf16[64,2,1536]{2,1,0:T(2,128)(2,1)}), bf16[64,2,1536]{2,1,0:T(2,128)(2,1)S(1)}, u32[]{:S(2)}, u32[]{:S(2)}) async-start(bf16[64,2,1536]{2,1,0:T(2,128)(2,1)} %reshape.143), calls=%async_computation.4 | async-start | bytes 786432 | tf_op jit(solution)/shard_map/all_to_all | solution.py:103
  897.4 66.2 %copy-start.6 = (bf16[1,24,64,128]{3,2,1,0:T(8,128)(2,1)S(1)}, bf16[1,24,64,128]{3,2,1,0:T(8,128)(2,1)}, u32[]{:S(2)}) copy-start(bf16[1,24,64,128]{3,2,1,0:T(8,128)(2,1)} %copy-done.5) | copy-start | bytes 1179652
  938.5 26.6 %copy-start.14 = (f32[24]{0:T(128)S(1)}, f32[24]{0:T(128)}, u32[]{:S(2)}) copy-start(f32[24]{0:T(128)} %get-tuple-element.50) | copy-start | bytes 292
  938.5 26.6 %copy-start.15 = (f32[24]{0:T(128)S(1)}, f32[24]{0:T(128)}, u32[]{:S(2)}) copy-start(f32[24]{0:T(128)} %get-tuple-element.51) | copy-start | bytes 292
  938.5 26.6 %copy-start.16 = (f32[24]{0:T(128)S(1)}, f32[24]{0:T(128)}, u32[]{:S(2)}) copy-start(f32[24]{0:T(128)} %get-tuple-element.52) | copy-start | bytes 292
  941.5 23.7 %copy-start.20 = (f32[24]{0:T(128)S(1)}, f32[24]{0:T(128)}, u32[]{:S(2)}) copy-start(f32[24]{0:T(128)} %get-tuple-element.56) | copy-start | bytes 292
  941.5 23.7 %copy-start.21 = (f32[24]{0:T(128)S(1)}, f32[24]{0:T(128)}, u32[]{:S(2)}) copy-start(f32[24]{0:T(128)} %get-tuple-element.57) | copy-start | bytes 292
  941.5 23.7 %copy-start.22 = (f32[24]{0:T(128)S(1)}, f32[24]{0:T(128)}, u32[]{:S(2)}) copy-start(f32[24]{0:T(128)} %get-tuple-element.58) | copy-start | bytes 292
  941.6 23.7 %copy-start.23 = (f32[24]{0:T(128)S(1)}, f32[24]{0:T(128)}, u32[]{:S(2)}) copy-start(f32[24]{0:T(128)} %get-tuple-element.59) | copy-start | bytes 292
  941.6 23.7 %copy-start.24 = (f32[24]{0:T(128)S(1)}, f32[24]{0:T(128)}, u32[]{:S(2)}) copy-start(f32[24]{0:T(128)} %get-tuple-element.60) | copy-start | bytes 292
  941.6 23.7 %copy-start.25 = (f32[24]{0:T(128)S(1)}, f32[24]{0:T(128)}, u32[]{:S(2)}) copy-start(f32[24]{0:T(128)} %get-tuple-element.61) | copy-start | bytes 292
  941.6 23.7 %copy-start.26 = (f32[24]{0:T(128)S(1)}, f32[24]{0:T(128)}, u32[]{:S(2)}) copy-start(f32[24]{0:T(128)} %get-tuple-element.62) | copy-start | bytes 292
  941.6 23.7 %copy-start.27 = (f32[24]{0:T(128)S(1)}, f32[24]{0:T(128)}, u32[]{:S(2)}) copy-start(f32[24]{0:T(128)} %get-tuple-element.63) | copy-start | bytes 292
  941.6 23.7 %copy-start.28 = (f32[24]{0:T(128)S(1)}, f32[24]{0:T(128)}, u32[]{:S(2)}) copy-start(f32[24]{0:T(128)} %get-tuple-element.64) | copy-start | bytes 292
  941.7 56.9 %copy-start.45 = (f32[24]{0:T(128)S(1)}, f32[24]{0:T(128)}, u32[]{:S(2)}) copy-start(f32[24]{0:T(128)} %get-tuple-element.88) | copy-start | bytes 292
  941.7 56.9 %copy-start.46 = (f32[24]{0:T(128)S(1)}, f32[24]{0:T(128)}, u32[]{:S(2)}) copy-start(f32[24]{0:T(128)} %get-tuple-element.89) | copy-start | bytes 292
  (29 other events, 467.9 us)
